TPU v7x, 128 devices: a whole 4x4x4 slice. The times are simulated.
128 devices in a mesh: gx: 16 (over z, y), gy: 8 (over x, core).
Axes of the slice: x: 4, y: 4, z: 4, core: 2. Of those that a mesh axis runs over, the one named last changes fastest.
Arguments:
- pumping: float32 [16, 4, 128, 1024], P(None, None, 'gx', 'gy'), may hold values from -1080 to 1080
- conductivity: float32 [4, 128, 1024], P(None, 'gx', 'gy'), may hold values from 0.2 to 5
- capacity: float32 [4, 128, 1024], P(None, 'gx', 'gy'), may hold values from 1 to 10
Outputs:
- solution: float32 [16, 4, 128, 1024], P(None, None, 'gx', 'gy')
- residual: float32 [16, 4, 128, 1024], P(None, None, 'gx', 'gy')
All inputs are finite; a program needn't handle non-finite values.
Results may differ from a plain program's by a relative error of at most 0.0035.
Values sent between devices are 32-bit elements; how exact they have to be, the bound alone decides.
A program may use at most 64 MiB of HBM per device.

v0:
```python
import jax
import jax.numpy as jnp
from jax import lax
from jax.sharding import PartitionSpec as P

RHS = 16
S = 4
CYCLES = 5
BASIS = 80


def padded_2(array, sides, width):
    for axis, dim in sides:
        devices, length = (lax.axis_size(axis), array.shape[dim])
        up = [(i, (i + 1) % devices) for i in range(devices - 1)]
        down = [(j, i) for i, j in up]
        last = lax.slice_in_dim(array, length - width, length, axis=dim)
        leading = lax.slice_in_dim(array, 0, width, axis=dim)
        before = lax.ppermute(last, axis, up)
        after = lax.ppermute(leading, axis, down)
        array = jnp.concatenate([before, array, after], axis=dim)
    return array


def halo_4(array):
    out = {}
    for axis, dim in (("gx", 2), ("gy", 3)):
        devices, length = (lax.axis_size(axis), array.shape[dim])
        up = [(i, (i + 1) % devices) for i in range(devices - 1)]
        down = [(j, i) for i, j in up]
        last = lax.slice_in_dim(array, length - 1, length, axis=dim)
        leading = lax.slice_in_dim(array, 0, 1, axis=dim)
        out[axis] = (lax.ppermute(last, axis, up), lax.ppermute(leading, axis, down))
    xb, xa = out["gx"]
    yb, ya = out["gy"]
    rows = jnp.concatenate([xb, array, xa], axis=2)
    zero_pad = ((0, 0), (0, 0), (1, 1), (0, 0))
    return jnp.concatenate([jnp.pad(yb, zero_pad), rows, jnp.pad(ya, zero_pad)], axis=3)


def face_terms(padded, storage):
    core = padded[1:-1, 1:-1, 1:-1]
    terms = (
        (core + padded[:-2, 1:-1, 1:-1]) * 0.5,
        (core + padded[2:, 1:-1, 1:-1]) * 0.5,
        (core + padded[1:-1, :-2, 1:-1]) * 0.5,
        (core + padded[1:-1, 2:, 1:-1]) * 0.5,
        (core + padded[1:-1, 1:-1, :-2]) * 0.5,
        (core + padded[1:-1, 1:-1, 2:]) * 0.5,
    )
    diagonal = storage + terms[0] + terms[1] + terms[2] + terms[3] + terms[4] + terms[5]
    return (terms, diagonal)


def apply_off(padded, terms):
    total = terms[0] * padded[:, :-2, 1:-1, 1:-1] + terms[1] * padded[:, 2:, 1:-1, 1:-1]
    total = total + terms[2] * padded[:, 1:-1, :-2, 1:-1] + terms[3] * padded[:, 1:-1, 2:, 1:-1]
    total = total + terms[4] * padded[:, 1:-1, 1:-1, :-2] + terms[5] * padded[:, 1:-1, 1:-1, 2:]
    return total


def small_solve(gram_all):
    shift_matrix = jnp.eye(BASIS, BASIS - RHS, dtype=jnp.float32) + jnp.eye(
        BASIS, BASIS - RHS, k=-RHS, dtype=jnp.float32
    )
    first_block = jnp.eye(BASIS, RHS, dtype=jnp.float32)
    hp = lax.Precision.HIGHEST
    gram_shift = jnp.dot(gram_all, shift_matrix, precision=hp)
    normal = jnp.dot(shift_matrix.T, gram_shift, precision=hp)
    right_side = jnp.dot(gram_shift.T, first_block, precision=hp)
    lower = jnp.linalg.cholesky(normal)
    y = jax.scipy.linalg.cho_solve((lower, True), right_side)
    coeffs = first_block - jnp.dot(shift_matrix, y, precision=hp)
    return (y, coeffs)


def shards(pumping, conductivity, capacity):
    hp = lax.Precision.HIGHEST
    shape = pumping.shape
    cond_halo = padded_2(conductivity, (("gx", 1), ("gy", 2)), 1)
    cond_pad = jnp.pad(cond_halo, ((1, 1), (0, 0), (0, 0)))
    terms, diagonal = face_terms(cond_pad, capacity)
    solution = jnp.zeros(shape, jnp.float32)
    residual = pumping / diagonal
    for restart in range(CYCLES):
        blocks = [residual]
        for k in range(S):
            bordered = halo_4(blocks[-1])
            padded = jnp.pad(bordered, ((0, 0), (1, 1), (0, 0), (0, 0)))
            blocks.append(-apply_off(padded, terms) / diagonal)
        stacked = jnp.concatenate(blocks, 0).reshape(BASIS, -1)
        local_gram = jnp.dot(stacked, stacked.T, precision=hp)
        gram_all = lax.psum(local_gram, ("gx", "gy"))
        y, coeffs = small_solve(gram_all)
        solution = solution + jnp.dot(y.T, stacked[: BASIS - RHS], precision=hp).reshape(shape)
        residual = jnp.dot(coeffs.T, stacked, precision=hp).reshape(shape)
    return (solution, residual)


def solution(mesh):
    return jax.shard_map(
        shards,
        mesh=mesh,
        in_specs=(P(None, None, "gx", "gy"), P(None, "gx", "gy"), P(None, "gx", "gy")),
        out_specs=(P(None, None, "gx", "gy"), P(None, None, "gx", "gy")),
        check_vma=False,
    )
```

profile of v0, /device:TPU:1, one launch (start us, length us, event | category | flops | bytes accessed | tf_op | source)
XLA Modules:
  0.0 819.0 jit_solution(14355877820562168291)
XLA Ops:
  1.4 4.0 collective-permute-start
  6.8 3.0 collective-permute-done.1
  10.6 5.1 collective-permute-start.2
  17.6 3.3 collective-permute-done.3
  23.9 3.2 collective-permute-start.5
  34.1 4.4 collective-permute-done.7
  39.3 4.3 collective-permute-start.9
  50.4 4.4 collective-permute-done.11
  55.6 5.2 collective-permute-start.13
  67.6 4.4 collective-permute-done.15
  72.9 4.3 collective-permute-start.17
  83.9 4.4 collective-permute-done.19
  90.7 75.5 %psum.35 = f32[80,80]{1,0:T(8,128)S(1)} all-reduce(f32[80,80]{1,0:T(8,128)S(1)} %convolution_bitcast_fusion.4), channel_id=1, replica_groups=mesh['gx'=16,'gy'=8] {'gx','gy'}, use_global_device_ids=true, to_apply=%region_0.1 | all-reduce | flops 6400 | bytes 51200 | tf_op jit(solution)/shard_map/psum | solution.py:93
  168.1 5.8 cholesky.89
  175.3 4.9 custom-call.11
  185.5 3.8 collective-permute-start.20
  192.7 4.4 collective-permute-done.23
  197.9 4.3 collective-permute-start.25
  209.0 4.4 collective-permute-done.27
  214.2 4.3 collective-permute-start.29
  225.2 4.4 collective-permute-done.31
  230.5 4.3 collective-permute-start.33
  238.2 2.5 collective-permute-start.35
  241.5 4.4 collective-permute-done.35
  249.4 73.8 %psum.36 = f32[80,80]{1,0:T(8,128)S(1)} all-reduce(f32[80,80]{1,0:T(8,128)S(1)} %convolution_bitcast_fusion.3), channel_id=1, replica_groups=mesh['gx'=16,'gy'=8] {'gx','gy'}, use_global_device_ids=true, to_apply=%region_3.6 | all-reduce | flops 6400 | bytes 51200 | tf_op jit(solution)/shard_map/psum | solution.py:93
  327.5 5.8 cholesky.100
  334.7 4.9 custom-call.12
  340.3 2.7 constant_dynamic-update-slice_fusion.11
  345.8 3.8 collective-permute-start.36
  352.9 4.4 collective-permute-done.39
  358.2 4.3 collective-permute-start.41
  369.2 4.4 collective-permute-done.43
  374.4 4.3 collective-permute-start.45
  385.5 4.4 collective-permute-done.47
  390.9 4.5 collective-permute-start.49
  403.6 2.8 collective-permute-done.51
  409.9 73.9 %psum.37 = f32[80,80]{1,0:T(8,128)S(1)} all-reduce(f32[80,80]{1,0:T(8,128)S(1)} %convolution_bitcast_fusion.2), channel_id=1, replica_groups=mesh['gx'=16,'gy'=8] {'gx','gy'}, use_global_device_ids=true, to_apply=%region_4.7 | all-reduce | flops 6400 | bytes 51200 | tf_op jit(solution)/shard_map/psum | solution.py:93
  488.1 5.8 cholesky.111
  495.3 4.9 custom-call.13
  500.9 2.8 constant_dynamic-update-slice_fusion.15
  506.5 4.3 collective-permute-start.52
  510.8 2.3 collective-permute-start.55
  514.4 4.1 collective-permute-done.55
  519.5 4.3 collective-permute-start.57
  531.0 3.8 collective-permute-done.59
  535.8 4.3 collective-permute-start.61
  546.9 4.2 collective-permute-done.63
  552.1 4.3 collective-permute-start.65
  564.5 2.8 collective-permute-done.67
  569.8 73.8 %psum.38 = f32[80,80]{1,0:T(8,128)S(1)} all-reduce(f32[80,80]{1,0:T(8,128)S(1)} %convolution_bitcast_fusion.1), channel_id=1, replica_groups=mesh['gx'=16,'gy'=8] {'gx','gy'}, use_global_device_ids=true, to_apply=%region_5.8 | all-reduce | flops 6400 | bytes 51200 | tf_op jit(solution)/shard_map/psum | solution.py:93
  645.5 5.8 cholesky.122
  652.7 4.9 custom-call.14
  662.6 4.1 collective-permute-start.68
  670.0 4.4 collective-permute-done.71
  675.4 4.3 collective-permute-start.73
  686.9 3.8 collective-permute-done.75
  691.6 4.3 collective-permute-start.77
  699.3 2.5 collective-permute-start.79
  703.0 3.9 collective-permute-done.79
  707.9 4.3 collective-permute-start.81
  719.5 3.8 collective-permute-done.83
  725.7 74.1 %psum.39 = f32[80,80]{1,0:T(8,128)S(1)} all-reduce(f32[80,80]{1,0:T(8,128)S(1)} %convolution_bitcast_fusion), channel_id=1, replica_groups=mesh['gx'=16,'gy'=8] {'gx','gy'}, use_global_device_ids=true, to_apply=%region_6.9 | all-reduce | flops 6400 | bytes 51200 | tf_op jit(solution)/shard_map/psum | solution.py:93
  801.7 5.8 cholesky.133
  808.9 4.9 custom-call.15
  (357 shorter events, 196.5 us)
Async XLA Ops:
  23.9 14.6 %collective-permute-start.5 = (f32[16,4,1,128]{3,0,2,1:T(8,128)S(1)}, f32[16,4,1,128]{3,0,2,1:T(8,128)S(1)}, u32[]{:S(2)}, u32[]{:S(2)}) collective-permute-start(f32[16,4,1,128]{3,0,2,1:T(8,128)S(1)} %get-tuple-element.125), channel_id=1, source_target_pairs={{0,8},{8,16},{16,24},{24,32},{32,40},{40,48},{48,56},{56,64},{64,7... | collective-permute-start | bytes 98312 | tf_op jit(solution)/shard_map/ppermute | solution.py:33
  27.1 11.4 %collective-permute-start.6 = (f32[16,4,1,128]{3,0,2,1:T(8,128)S(1)}, f32[16,4,1,128]{3,0,2,1:T(8,128)S(1)}, u32[]{:S(2)}, u32[]{:S(2)}) collective-permute-start(f32[16,4,1,128]{3,0,2,1:T(8,128)S(1)} %get-tuple-element.126), channel_id=1, source_target_pairs={{8,0},{16,8},{24,16},{32,24},{40,32},{48,40},{56,48},{64,56},{72,6... | collective-permute-start | bytes 98312 | tf_op jit(solution)/shard_map/ppermute | solution.py:33
  30.8 7.7 collective-permute-start.7
  39.3 15.5 %collective-permute-start.9 = (f32[16,4,1,128]{3,0,2,1:T(8,128)S(1)}, f32[16,4,1,128]{3,0,2,1:T(8,128)S(1)}, u32[]{:S(2)}, u32[]{:S(2)}) collective-permute-start(f32[16,4,1,128]{3,0,2,1:T(8,128)S(1)} %get-tuple-element.121), channel_id=1, source_target_pairs={{0,8},{8,16},{16,24},{24,32},{32,40},{40,48},{48,56},{56,64},{64,7... | collective-permute-start | bytes 98312 | tf_op jit(solution)/shard_map/ppermute | solution.py:33
  43.6 11.2 %collective-permute-start.10 = (f32[16,4,1,128]{3,0,2,1:T(8,128)S(1)}, f32[16,4,1,128]{3,0,2,1:T(8,128)S(1)}, u32[]{:S(2)}, u32[]{:S(2)}) collective-permute-start(f32[16,4,1,128]{3,0,2,1:T(8,128)S(1)} %get-tuple-element.122), channel_id=1, source_target_pairs={{8,0},{16,8},{24,16},{32,24},{40,32},{48,40},{56,48},{64,56},{72,6... | collective-permute-start | bytes 98312 | tf_op jit(solution)/shard_map/ppermute | solution.py:33
  47.0 7.7 collective-permute-start.11
  55.6 16.4 %collective-permute-start.13 = (f32[16,4,1,128]{3,0,2,1:T(8,128)S(1)}, f32[16,4,1,128]{3,0,2,1:T(8,128)S(1)}, u32[]{:S(2)}, u32[]{:S(2)}) collective-permute-start(f32[16,4,1,128]{3,0,2,1:T(8,128)S(1)} %get-tuple-element.117), channel_id=1, source_target_pairs={{0,8},{8,16},{16,24},{24,32},{32,40},{40,48},{48,56},{56,64},{64,7... | collective-permute-start | bytes 98312 | tf_op jit(solution)/shard_map/ppermute | solution.py:33
  60.8 11.2 %collective-permute-start.14 = (f32[16,4,1,128]{3,0,2,1:T(8,128)S(1)}, f32[16,4,1,128]{3,0,2,1:T(8,128)S(1)}, u32[]{:S(2)}, u32[]{:S(2)}) collective-permute-start(f32[16,4,1,128]{3,0,2,1:T(8,128)S(1)} %get-tuple-element.118), channel_id=1, source_target_pairs={{8,0},{16,8},{24,16},{32,24},{40,32},{48,40},{56,48},{64,56},{72,6... | collective-permute-start | bytes 98312 | tf_op jit(solution)/shard_map/ppermute | solution.py:33
  64.3 7.7 collective-permute-start.15
  72.9 15.3 %collective-permute-start.17 = (f32[16,4,1,128]{3,0,2,1:T(8,128)S(1)}, f32[16,4,1,128]{3,0,2,1:T(8,128)S(1)}, u32[]{:S(2)}, u32[]{:S(2)}) collective-permute-start(f32[16,4,1,128]{3,0,2,1:T(8,128)S(1)} %get-tuple-element.113), channel_id=1, source_target_pairs={{0,8},{8,16},{16,24},{24,32},{32,40},{40,48},{48,56},{56,64},{64,7... | collective-permute-start | bytes 98312 | tf_op jit(solution)/shard_map/ppermute | solution.py:33
  77.2 11.1 %collective-permute-start.18 = (f32[16,4,1,128]{3,0,2,1:T(8,128)S(1)}, f32[16,4,1,128]{3,0,2,1:T(8,128)S(1)}, u32[]{:S(2)}, u32[]{:S(2)}) collective-permute-start(f32[16,4,1,128]{3,0,2,1:T(8,128)S(1)} %get-tuple-element.114), channel_id=1, source_target_pairs={{8,0},{16,8},{24,16},{32,24},{40,32},{48,40},{56,48},{64,56},{72,6... | collective-permute-start | bytes 98312 | tf_op jit(solution)/shard_map/ppermute | solution.py:33
  80.6 7.7 collective-permute-start.19
  182.4 14.7 %collective-permute-start.21 = (f32[16,4,1,128]{3,0,2,1:T(8,128)S(1)}, f32[16,4,1,128]{3,0,2,1:T(8,128)S(1)}, u32[]{:S(2)}, u32[]{:S(2)}) collective-permute-start(f32[16,4,1,128]{3,0,2,1:T(8,128)S(1)} %get-tuple-element.109), channel_id=1, source_target_pairs={{0,8},{8,16},{16,24},{24,32},{32,40},{40,48},{48,56},{56,64},{64,7... | collective-permute-start | bytes 98312 | tf_op jit(solution)/shard_map/ppermute | solution.py:33
  184.1 13.0 %collective-permute-start.22 = (f32[16,4,1,128]{3,0,2,1:T(8,128)S(1)}, f32[16,4,1,128]{3,0,2,1:T(8,128)S(1)}, u32[]{:S(2)}, u32[]{:S(2)}) collective-permute-start(f32[16,4,1,128]{3,0,2,1:T(8,128)S(1)} %get-tuple-element.110), channel_id=1, source_target_pairs={{8,0},{16,8},{24,16},{32,24},{40,32},{48,40},{56,48},{64,56},{72,6... | collective-permute-start | bytes 98312 | tf_op jit(solution)/shard_map/ppermute | solution.py:33
  185.5 7.1 collective-permute-start.20
  189.4 7.7 collective-permute-start.23
  197.9 15.5 %collective-permute-start.25 = (f32[16,4,1,128]{3,0,2,1:T(8,128)S(1)}, f32[16,4,1,128]{3,0,2,1:T(8,128)S(1)}, u32[]{:S(2)}, u32[]{:S(2)}) collective-permute-start(f32[16,4,1,128]{3,0,2,1:T(8,128)S(1)} %get-tuple-element.105), channel_id=1, source_target_pairs={{0,8},{8,16},{16,24},{24,32},{32,40},{40,48},{48,56},{56,64},{64,7... | collective-permute-start | bytes 98312 | tf_op jit(solution)/shard_map/ppermute | solution.py:33
  202.2 11.2 %collective-permute-start.26 = (f32[16,4,1,128]{3,0,2,1:T(8,128)S(1)}, f32[16,4,1,128]{3,0,2,1:T(8,128)S(1)}, u32[]{:S(2)}, u32[]{:S(2)}) collective-permute-start(f32[16,4,1,128]{3,0,2,1:T(8,128)S(1)} %get-tuple-element.106), channel_id=1, source_target_pairs={{8,0},{16,8},{24,16},{32,24},{40,32},{48,40},{56,48},{64,56},{72,6... | collective-permute-start | bytes 98312 | tf_op jit(solution)/shard_map/ppermute | solution.py:33
  205.6 7.7 collective-permute-start.27
  214.2 15.5 %collective-permute-start.29 = (f32[16,4,1,128]{3,0,2,1:T(8,128)S(1)}, f32[16,4,1,128]{3,0,2,1:T(8,128)S(1)}, u32[]{:S(2)}, u32[]{:S(2)}) collective-permute-start(f32[16,4,1,128]{3,0,2,1:T(8,128)S(1)} %get-tuple-element.101), channel_id=1, source_target_pairs={{0,8},{8,16},{16,24},{24,32},{32,40},{40,48},{48,56},{56,64},{64,7... | collective-permute-start | bytes 98312 | tf_op jit(solution)/shard_map/ppermute | solution.py:33
  218.4 11.2 %collective-permute-start.30 = (f32[16,4,1,128]{3,0,2,1:T(8,128)S(1)}, f32[16,4,1,128]{3,0,2,1:T(8,128)S(1)}, u32[]{:S(2)}, u32[]{:S(2)}) collective-permute-start(f32[16,4,1,128]{3,0,2,1:T(8,128)S(1)} %get-tuple-element.102), channel_id=1, source_target_pairs={{8,0},{16,8},{24,16},{32,24},{40,32},{48,40},{56,48},{64,56},{72,6... | collective-permute-start | bytes 98312 | tf_op jit(solution)/shard_map/ppermute | solution.py:33
  221.9 7.7 collective-permute-start.31
  230.5 15.5 %collective-permute-start.33 = (f32[16,4,1,128]{3,0,2,1:T(8,128)S(1)}, f32[16,4,1,128]{3,0,2,1:T(8,128)S(1)}, u32[]{:S(2)}, u32[]{:S(2)}) collective-permute-start(f32[16,4,1,128]{3,0,2,1:T(8,128)S(1)} %get-tuple-element.97), channel_id=1, source_target_pairs={{0,8},{8,16},{16,24},{24,32},{32,40},{40,48},{48,56},{56,64},{64,7... | collective-permute-start | bytes 98312 | tf_op jit(solution)/shard_map/ppermute | solution.py:33
  234.7 11.2 %collective-permute-start.34 = (f32[16,4,1,128]{3,0,2,1:T(8,128)S(1)}, f32[16,4,1,128]{3,0,2,1:T(8,128)S(1)}, u32[]{:S(2)}, u32[]{:S(2)}) collective-permute-start(f32[16,4,1,128]{3,0,2,1:T(8,128)S(1)} %get-tuple-element.98), channel_id=1, source_target_pairs={{8,0},{16,8},{24,16},{32,24},{40,32},{48,40},{56,48},{64,56},{72,6... | collective-permute-start | bytes 98312 | tf_op jit(solution)/shard_map/ppermute | solution.py:33
  238.2 7.7 collective-permute-start.35
  343.1 14.3 %collective-permute-start.37 = (f32[16,4,1,128]{3,0,2,1:T(8,128)S(1)}, f32[16,4,1,128]{3,0,2,1:T(8,128)S(1)}, u32[]{:S(2)}, u32[]{:S(2)}) collective-permute-start(f32[16,4,1,128]{3,0,2,1:T(8,128)S(1)} %get-tuple-element.93), channel_id=1, source_target_pairs={{0,8},{8,16},{16,24},{24,32},{32,40},{40,48},{48,56},{56,64},{64,7... | collective-permute-start | bytes 98312 | tf_op jit(solution)/shard_map/ppermute | solution.py:33
  344.4 13.0 %collective-permute-start.38 = (f32[16,4,1,128]{3,0,2,1:T(8,128)S(1)}, f32[16,4,1,128]{3,0,2,1:T(8,128)S(1)}, u32[]{:S(2)}, u32[]{:S(2)}) collective-permute-start(f32[16,4,1,128]{3,0,2,1:T(8,128)S(1)} %get-tuple-element.94), channel_id=1, source_target_pairs={{8,0},{16,8},{24,16},{32,24},{40,32},{48,40},{56,48},{64,56},{72,6... | collective-permute-start | bytes 98312 | tf_op jit(solution)/shard_map/ppermute | solution.py:33
  345.8 7.1 collective-permute-start.36
  349.6 7.7 collective-permute-start.39
  358.2 15.5 %collective-permute-start.41 = (f32[16,4,1,128]{3,0,2,1:T(8,128)S(1)}, f32[16,4,1,128]{3,0,2,1:T(8,128)S(1)}, u32[]{:S(2)}, u32[]{:S(2)}) collective-permute-start(f32[16,4,1,128]{3,0,2,1:T(8,128)S(1)} %get-tuple-element.89), channel_id=1, source_target_pairs={{0,8},{8,16},{16,24},{24,32},{32,40},{40,48},{48,56},{56,64},{64,7... | collective-permute-start | bytes 98312 | tf_op jit(solution)/shard_map/ppermute | solution.py:33
  362.4 11.2 %collective-permute-start.42 = (f32[16,4,1,128]{3,0,2,1:T(8,128)S(1)}, f32[16,4,1,128]{3,0,2,1:T(8,128)S(1)}, u32[]{:S(2)}, u32[]{:S(2)}) collective-permute-start(f32[16,4,1,128]{3,0,2,1:T(8,128)S(1)} %get-tuple-element.90), channel_id=1, source_target_pairs={{8,0},{16,8},{24,16},{32,24},{40,32},{48,40},{56,48},{64,56},{72,6... | collective-permute-start | bytes 98312 | tf_op jit(solution)/shard_map/ppermute | solution.py:33
  365.9 7.7 collective-permute-start.43
  374.4 15.5 %collective-permute-start.45 = (f32[16,4,1,128]{3,0,2,1:T(8,128)S(1)}, f32[16,4,1,128]{3,0,2,1:T(8,128)S(1)}, u32[]{:S(2)}, u32[]{:S(2)}) collective-permute-start(f32[16,4,1,128]{3,0,2,1:T(8,128)S(1)} %get-tuple-element.85), channel_id=1, source_target_pairs={{0,8},{8,16},{16,24},{24,32},{32,40},{40,48},{48,56},{56,64},{64,7... | collective-permute-start | bytes 98312 | tf_op jit(solution)/shard_map/ppermute | solution.py:33
  378.7 11.2 %collective-permute-start.46 = (f32[16,4,1,128]{3,0,2,1:T(8,128)S(1)}, f32[16,4,1,128]{3,0,2,1:T(8,128)S(1)}, u32[]{:S(2)}, u32[]{:S(2)}) collective-permute-start(f32[16,4,1,128]{3,0,2,1:T(8,128)S(1)} %get-tuple-element.86), channel_id=1, source_target_pairs={{8,0},{16,8},{24,16},{32,24},{40,32},{48,40},{56,48},{64,56},{72,6... | collective-permute-start | bytes 98312 | tf_op jit(solution)/shard_map/ppermute | solution.py:33
  382.2 7.7 collective-permute-start.47
  390.9 15.5 %collective-permute-start.49 = (f32[16,4,1,128]{3,0,2,1:T(8,128)S(1)}, f32[16,4,1,128]{3,0,2,1:T(8,128)S(1)}, u32[]{:S(2)}, u32[]{:S(2)}) collective-permute-start(f32[16,4,1,128]{3,0,2,1:T(8,128)S(1)} %get-tuple-element.81), channel_id=1, source_target_pairs={{0,8},{8,16},{16,24},{24,32},{32,40},{40,48},{48,56},{56,64},{64,7... | collective-permute-start | bytes 98312 | tf_op jit(solution)/shard_map/ppermute | solution.py:33
  395.3 11.1 %collective-permute-start.50 = (f32[16,4,1,128]{3,0,2,1:T(8,128)S(1)}, f32[16,4,1,128]{3,0,2,1:T(8,128)S(1)}, u32[]{:S(2)}, u32[]{:S(2)}) collective-permute-start(f32[16,4,1,128]{3,0,2,1:T(8,128)S(1)} %get-tuple-element.82), channel_id=1, source_target_pairs={{8,0},{16,8},{24,16},{32,24},{40,32},{48,40},{56,48},{64,56},{72,6... | collective-permute-start | bytes 98312 | tf_op jit(solution)/shard_map/ppermute | solution.py:33
  398.7 7.7 collective-permute-start.51
  503.9 14.7 %collective-permute-start.53 = (f32[16,4,1,128]{3,0,2,1:T(8,128)S(1)}, f32[16,4,1,128]{3,0,2,1:T(8,128)S(1)}, u32[]{:S(2)}, u32[]{:S(2)}) collective-permute-start(f32[16,4,1,128]{3,0,2,1:T(8,128)S(1)} %get-tuple-element.77), channel_id=1, source_target_pairs={{0,8},{8,16},{16,24},{24,32},{32,40},{40,48},{48,56},{56,64},{64,7... | collective-permute-start | bytes 98312 | tf_op jit(solution)/shard_map/ppermute | solution.py:33
  505.2 13.4 %collective-permute-start.54 = (f32[16,4,1,128]{3,0,2,1:T(8,128)S(1)}, f32[16,4,1,128]{3,0,2,1:T(8,128)S(1)}, u32[]{:S(2)}, u32[]{:S(2)}) collective-permute-start(f32[16,4,1,128]{3,0,2,1:T(8,128)S(1)} %get-tuple-element.78), channel_id=1, source_target_pairs={{8,0},{16,8},{24,16},{32,24},{40,32},{48,40},{56,48},{64,56},{72,6... | collective-permute-start | bytes 98312 | tf_op jit(solution)/shard_map/ppermute | solution.py:33
  506.5 7.9 collective-permute-start.52
  510.8 7.7 collective-permute-start.55
  519.5 15.3 %collective-permute-start.57 = (f32[16,4,1,128]{3,0,2,1:T(8,128)S(1)}, f32[16,4,1,128]{3,0,2,1:T(8,128)S(1)}, u32[]{:S(2)}, u32[]{:S(2)}) collective-permute-start(f32[16,4,1,128]{3,0,2,1:T(8,128)S(1)} %get-tuple-element.73), channel_id=1, source_target_pairs={{0,8},{8,16},{16,24},{24,32},{32,40},{40,48},{48,56},{56,64},{64,7... | collective-permute-start | bytes 98312 | tf_op jit(solution)/shard_map/ppermute | solution.py:33
  523.8 11.1 %collective-permute-start.58 = (f32[16,4,1,128]{3,0,2,1:T(8,128)S(1)}, f32[16,4,1,128]{3,0,2,1:T(8,128)S(1)}, u32[]{:S(2)}, u32[]{:S(2)}) collective-permute-start(f32[16,4,1,128]{3,0,2,1:T(8,128)S(1)} %get-tuple-element.74), channel_id=1, source_target_pairs={{8,0},{16,8},{24,16},{32,24},{40,32},{48,40},{56,48},{64,56},{72,6... | collective-permute-start | bytes 98312 | tf_op jit(solution)/shard_map/ppermute | solution.py:33
  527.1 7.7 collective-permute-start.59
  535.8 15.3 %collective-permute-start.61 = (f32[16,4,1,128]{3,0,2,1:T(8,128)S(1)}, f32[16,4,1,128]{3,0,2,1:T(8,128)S(1)}, u32[]{:S(2)}, u32[]{:S(2)}) collective-permute-start(f32[16,4,1,128]{3,0,2,1:T(8,128)S(1)} %get-tuple-element.69), channel_id=1, source_target_pairs={{0,8},{8,16},{16,24},{24,32},{32,40},{40,48},{48,56},{56,64},{64,7... | collective-permute-start | bytes 98312 | tf_op jit(solution)/shard_map/ppermute | solution.py:33
  540.0 11.1 %collective-permute-start.62 = (f32[16,4,1,128]{3,0,2,1:T(8,128)S(1)}, f32[16,4,1,128]{3,0,2,1:T(8,128)S(1)}, u32[]{:S(2)}, u32[]{:S(2)}) collective-permute-start(f32[16,4,1,128]{3,0,2,1:T(8,128)S(1)} %get-tuple-element.70), channel_id=1, source_target_pairs={{8,0},{16,8},{24,16},{32,24},{40,32},{48,40},{56,48},{64,56},{72,6... | collective-permute-start | bytes 98312 | tf_op jit(solution)/shard_map/ppermute | solution.py:33
  543.4 7.7 collective-permute-start.63
  552.1 15.3 %collective-permute-start.65 = (f32[16,4,1,128]{3,0,2,1:T(8,128)S(1)}, f32[16,4,1,128]{3,0,2,1:T(8,128)S(1)}, u32[]{:S(2)}, u32[]{:S(2)}) collective-permute-start(f32[16,4,1,128]{3,0,2,1:T(8,128)S(1)} %get-tuple-element.65), channel_id=1, source_target_pairs={{0,8},{8,16},{16,24},{24,32},{32,40},{40,48},{48,56},{56,64},{64,7... | collective-permute-start | bytes 98312 | tf_op jit(solution)/shard_map/ppermute | solution.py:33
  556.3 11.1 %collective-permute-start.66 = (f32[16,4,1,128]{3,0,2,1:T(8,128)S(1)}, f32[16,4,1,128]{3,0,2,1:T(8,128)S(1)}, u32[]{:S(2)}, u32[]{:S(2)}) collective-permute-start(f32[16,4,1,128]{3,0,2,1:T(8,128)S(1)} %get-tuple-element.66), channel_id=1, source_target_pairs={{8,0},{16,8},{24,16},{32,24},{40,32},{48,40},{56,48},{64,56},{72,6... | collective-permute-start | bytes 98312 | tf_op jit(solution)/shard_map/ppermute | solution.py:33
  559.7 7.7 collective-permute-start.67
  660.0 14.4 %collective-permute-start.69 = (f32[16,4,1,128]{3,0,2,1:T(8,128)S(1)}, f32[16,4,1,128]{3,0,2,1:T(8,128)S(1)}, u32[]{:S(2)}, u32[]{:S(2)}) collective-permute-start(f32[16,4,1,128]{3,0,2,1:T(8,128)S(1)} %get-tuple-element.61), channel_id=1, source_target_pairs={{0,8},{8,16},{16,24},{24,32},{32,40},{40,48},{48,56},{56,64},{64,7... | collective-permute-start | bytes 98312 | tf_op jit(solution)/shard_map/ppermute | solution.py:33
  661.3 13.2 %collective-permute-start.70 = (f32[16,4,1,128]{3,0,2,1:T(8,128)S(1)}, f32[16,4,1,128]{3,0,2,1:T(8,128)S(1)}, u32[]{:S(2)}, u32[]{:S(2)}) collective-permute-start(f32[16,4,1,128]{3,0,2,1:T(8,128)S(1)} %get-tuple-element.62), channel_id=1, source_target_pairs={{8,0},{16,8},{24,16},{32,24},{40,32},{48,40},{56,48},{64,56},{72,6... | collective-permute-start | bytes 98312 | tf_op jit(solution)/shard_map/ppermute | solution.py:33
  662.6 7.4 collective-permute-start.68
  666.7 7.7 collective-permute-start.71
  675.4 15.3 %collective-permute-start.73 = (f32[16,4,1,128]{3,0,2,1:T(8,128)S(1)}, f32[16,4,1,128]{3,0,2,1:T(8,128)S(1)}, u32[]{:S(2)}, u32[]{:S(2)}) collective-permute-start(f32[16,4,1,128]{3,0,2,1:T(8,128)S(1)} %get-tuple-element.57), channel_id=1, source_target_pairs={{0,8},{8,16},{16,24},{24,32},{32,40},{40,48},{48,56},{56,64},{64,7... | collective-permute-start | bytes 98312 | tf_op jit(solution)/shard_map/ppermute | solution.py:33
  679.6 11.1 %collective-permute-start.74 = (f32[16,4,1,128]{3,0,2,1:T(8,128)S(1)}, f32[16,4,1,128]{3,0,2,1:T(8,128)S(1)}, u32[]{:S(2)}, u32[]{:S(2)}) collective-permute-start(f32[16,4,1,128]{3,0,2,1:T(8,128)S(1)} %get-tuple-element.58), channel_id=1, source_target_pairs={{8,0},{16,8},{24,16},{32,24},{40,32},{48,40},{56,48},{64,56},{72,6... | collective-permute-start | bytes 98312 | tf_op jit(solution)/shard_map/ppermute | solution.py:33
  683.0 7.7 collective-permute-start.75
  691.6 15.3 %collective-permute-start.77 = (f32[16,4,1,128]{3,0,2,1:T(8,128)S(1)}, f32[16,4,1,128]{3,0,2,1:T(8,128)S(1)}, u32[]{:S(2)}, u32[]{:S(2)}) collective-permute-start(f32[16,4,1,128]{3,0,2,1:T(8,128)S(1)} %get-tuple-element.53), channel_id=1, source_target_pairs={{0,8},{8,16},{16,24},{24,32},{32,40},{40,48},{48,56},{56,64},{64,7... | collective-permute-start | bytes 98312 | tf_op jit(solution)/shard_map/ppermute | solution.py:33
  695.9 11.1 %collective-permute-start.78 = (f32[16,4,1,128]{3,0,2,1:T(8,128)S(1)}, f32[16,4,1,128]{3,0,2,1:T(8,128)S(1)}, u32[]{:S(2)}, u32[]{:S(2)}) collective-permute-start(f32[16,4,1,128]{3,0,2,1:T(8,128)S(1)} %get-tuple-element.54), channel_id=1, source_target_pairs={{8,0},{16,8},{24,16},{32,24},{40,32},{48,40},{56,48},{64,56},{72,6... | collective-permute-start | bytes 98312 | tf_op jit(solution)/shard_map/ppermute | solution.py:33
  699.3 7.7 collective-permute-start.79
  707.9 15.3 %collective-permute-start.81 = (f32[16,4,1,128]{3,0,2,1:T(8,128)S(1)}, f32[16,4,1,128]{3,0,2,1:T(8,128)S(1)}, u32[]{:S(2)}, u32[]{:S(2)}) collective-permute-start(f32[16,4,1,128]{3,0,2,1:T(8,128)S(1)} %get-tuple-element.49), channel_id=1, source_target_pairs={{0,8},{8,16},{16,24},{24,32},{32,40},{40,48},{48,56},{56,64},{64,7... | collective-permute-start | bytes 98312 | tf_op jit(solution)/shard_map/ppermute | solution.py:33
  712.2 11.1 %collective-permute-start.82 = (f32[16,4,1,128]{3,0,2,1:T(8,128)S(1)}, f32[16,4,1,128]{3,0,2,1:T(8,128)S(1)}, u32[]{:S(2)}, u32[]{:S(2)}) collective-permute-start(f32[16,4,1,128]{3,0,2,1:T(8,128)S(1)} %get-tuple-element.50), channel_id=1, source_target_pairs={{8,0},{16,8},{24,16},{32,24},{40,32},{48,40},{56,48},{64,56},{72,6... | collective-permute-start | bytes 98312 | tf_op jit(solution)/shard_map/ppermute | solution.py:33
  715.5 7.7 collective-permute-start.83
  (22 other events, 135.4 us)
where the time goes:
time: 827 us; the launch traced here: 819 us
  blocking collectives  371 us (45%)
  starting transfers between devices  206 us (25%)
  waiting for transfers between devices  99.7 us (12%)
  other arithmetic  80.1 us (10%)
  local copies, waits for them, and re-layouts  29.8 us (4%)
  matrix products  28.9 us (3%)
    psum x5, blocking collectives, shards(): gram_all = lax.psum(local_gram, ('gx', 'gy'))  371 us
    ppermute x40, starting transfers between devices, halo_4(): lax.ppermute(last, axis, up)  123 us
    ppermute x40, waiting for transfers between devices, halo_4(): lax.ppermute(leading, axis, down)  81.7 us
    ppermute x40, starting transfers between devices, halo_4(): lax.ppermute(leading, axis, down)  71.1 us
    another operation x15, other arithmetic, small_solve(): lower = jnp.linalg.cholesky(normal)  32.6 us
    another operation x10, other arithmetic, small_solve(): y = jax.scipy.linalg.cho_solve((lower, True), right_side)  27.7 us
    unnamed x26, local copies, waits for them, and re-layouts  17.6 us
  transfers between devices with their start and end apart: 84, of which 34 were waited for; matrix products, arithmetic and copies ran while one was open for 2% of the time, Pallas kernels for 0%

commit v1 on v0

--- a/solution.py
+++ b/solution.py
@@ -90,7 +90,7 @@
             blocks.append(-apply_off(padded, terms) / diagonal)
         stacked = jnp.concatenate(blocks, 0).reshape(BASIS, -1)
         local_gram = jnp.dot(stacked, stacked.T, precision=hp)
-        gram_all = lax.psum(local_gram, ("gx", "gy"))
+        gram_all = jnp.sum(lax.all_gather(local_gram, ("gx", "gy")), axis=0)
         y, coeffs = small_solve(gram_all)
         solution = solution + jnp.dot(y.T, stacked[: BASIS - RHS], precision=hp).reshape(shape)
         residual = jnp.dot(coeffs.T, stacked, precision=hp).reshape(shape)

time: 827 us -> 849 us (1.027)
  blocking collectives: 371 us -> 0 us
  waiting for transfers between devices: 99.7 us -> 463 us
  other arithmetic: 80.1 us -> 95.2 us
  between operations: 3.35 us -> 16.7 us
    psum x5 -> x0, blocking collectives: 371 us -> none  [shards(): gram_all = lax.psum(local_gram, ('gx', 'gy'))]
    all_gather x0 -> x5, waiting for transfers between devices: none -> 348 us  [shards(): gram_all = jnp.sum(lax.all_gather(local_gram, ('gx', 'gy')), axis=0)]
    reduce_sum x0 -> x5, other arithmetic: none -> 14.5 us  [shards(): gram_all = jnp.sum(lax.all_gather(local_gram, ('gx', 'gy')), axis=0)]
    ppermute x40, waiting for transfers between devices: 11.8 us -> 21.1 us  [halo_4(): lax.ppermute(last, axis, up)]
    unnamed x26 -> x74, local copies, waits for them, and re-layouts: 17.6 us -> 17.4 us
  transfers between devices with their start and end apart: 84 -> 89, of which waited for: 34 -> 47; matrix products, arithmetic and copies ran while one was open for 2% -> 4% of each run, Pallas kernels for 0% -> 0%
where the time goes in v1:
time: 849 us; the launch traced here: 841 us
  waiting for transfers between devices  463 us (55%)
  starting transfers between devices  203 us (24%)
  other arithmetic  95.2 us (11%)
  matrix products  35.4 us (4%)
  local copies, waits for them, and re-layouts  27.5 us (3%)
  between operations  16.7 us (2%)
    all_gather x5, waiting for transfers between devices, shards(): gram_all = jnp.sum(lax.all_gather(local_gram, ('gx', 'gy')), axis=0)  348 us
    ppermute x40, starting transfers between devices, halo_4(): lax.ppermute(last, axis, up)  119 us
    ppermute x40, waiting for transfers between devices, halo_4(): lax.ppermute(leading, axis, down)  87.4 us
    ppermute x40, starting transfers between devices, halo_4(): lax.ppermute(leading, axis, down)  70.5 us
    another operation x15, other arithmetic, small_solve(): lower = jnp.linalg.cholesky(normal)  32.6 us
    another operation x10, other arithmetic, small_solve(): y = jax.scipy.linalg.cho_solve((lower, True), right_side)  27.4 us
    ppermute x40, waiting for transfers between devices, halo_4(): lax.ppermute(last, axis, up)  21.1 us
    unnamed x74, local copies, waits for them, and re-layouts  17.4 us
  transfers between devices with their start and end apart: 89, of which 47 were waited for; matrix products, arithmetic and copies ran while one was open for 4% of the time, Pallas kernels for 0%

profile of v1, /device:TPU:1, one launch (start us, length us, event | category | flops | bytes accessed | tf_op | source)
XLA Modules:
  0.0 840.8 jit_solution(17181096815266075589)
XLA Ops:
  8.0 4.0 collective-permute-start
  13.3 3.0 collective-permute-done.1
  17.2 5.1 collective-permute-start.2
  24.2 3.3 collective-permute-done.3
  30.5 3.2 collective-permute-start.5
  40.7 4.4 collective-permute-done.7
  45.9 4.3 collective-permute-start.9
  56.9 4.4 collective-permute-done.11
  62.2 5.2 collective-permute-start.13
  74.2 4.4 collective-permute-done.15
  79.4 4.3 collective-permute-start.17
  90.5 4.4 collective-permute-done.19
  100.7 72.9 %all-gather.11.cloned.1.call-done = f32[10240,80]{1,0:T(8,128)} async-done(((f32[80,80]{1,0:T(8,128)}), f32[10240,80]{1,0:T(8,128)}) %all-gather.11.cloned.1.call-update) | async-done | bytes 3276816 | tf_op jit(solution)/shard_map/all_gather | solution.py:93
  173.6 2.9 reduce_sum.45
  177.4 5.8 cholesky.89
  184.5 4.9 custom-call.11
  196.1 2.8 collective-permute-start.20
  202.2 4.4 collective-permute-done.23
  207.4 4.3 collective-permute-start.25
  218.5 4.4 collective-permute-done.27
  223.7 4.3 collective-permute-start.29
  234.8 4.4 collective-permute-done.31
  240.0 4.3 collective-permute-start.33
  251.1 4.4 collective-permute-done.35
  261.0 72.4 %all-gather.13.cloned.1.call-done = f32[10240,80]{1,0:T(8,128)} async-done(((f32[80,80]{1,0:T(8,128)}), f32[10240,80]{1,0:T(8,128)}) %all-gather.13.cloned.1.call-update) | async-done | bytes 3276816 | tf_op jit(solution)/shard_map/all_gather | solution.py:93
  333.4 2.9 reduce_sum.46
  337.2 5.8 cholesky.100
  344.3 4.9 custom-call.12
  355.9 2.8 collective-permute-start.36
  362.0 4.4 collective-permute-done.39
  367.2 4.3 collective-permute-start.41
  378.3 4.4 collective-permute-done.43
  383.5 4.3 collective-permute-start.45
  394.6 4.4 collective-permute-done.47
  399.8 4.3 collective-permute-start.49
  410.9 4.4 collective-permute-done.51
  420.8 72.4 %all-gather.15.cloned.1.call-done = f32[10240,80]{1,0:T(8,128)} async-done(((f32[80,80]{1,0:T(8,128)}), f32[10240,80]{1,0:T(8,128)}) %all-gather.15.cloned.1.call-update) | async-done | bytes 3276816 | tf_op jit(solution)/shard_map/all_gather | solution.py:93
  493.2 2.9 reduce_sum.47
  497.0 5.8 cholesky.111
  504.1 4.9 custom-call.13
  515.7 2.8 collective-permute-start.52
  521.8 4.4 collective-permute-done.55
  527.0 4.3 collective-permute-start.57
  538.1 4.4 collective-permute-done.59
  543.3 4.3 collective-permute-start.61
  554.4 4.4 collective-permute-done.63
  559.6 4.3 collective-permute-start.65
  570.7 4.4 collective-permute-done.67
  580.8 72.2 %all-gather.17.cloned.1.call-done = f32[10240,80]{1,0:T(8,128)} async-done(((f32[80,80]{1,0:T(8,128)}), f32[10240,80]{1,0:T(8,128)}) %all-gather.17.cloned.1.call-update) | async-done | bytes 3276816 | tf_op jit(solution)/shard_map/all_gather | solution.py:93
  653.0 2.9 reduce_sum.48
  656.8 5.8 cholesky.122
  663.9 4.9 custom-call.14
  675.9 2.8 collective-permute-start.68
  681.9 4.4 collective-permute-done.71
  687.2 4.3 collective-permute-start.73
  698.2 4.4 collective-permute-done.75
  703.5 4.3 collective-permute-start.77
  714.5 4.4 collective-permute-done.79
  719.8 4.3 collective-permute-start.81
  730.9 4.4 collective-permute-done.83
  755.4 57.8 %all-gather.19.cloned.1.call-done = f32[10240,80]{1,0:T(8,128)} async-done(((f32[80,80]{1,0:T(8,128)}), f32[10240,80]{1,0:T(8,128)}) %all-gather.19.cloned.1.call-update) | async-done | bytes 3276816 | tf_op jit(solution)/shard_map/all_gather | solution.py:93
  813.2 2.9 reduce_sum.49
  817.0 5.8 cholesky.133
  824.2 4.9 custom-call.15
  (420 shorter events, 226.1 us)
Async XLA Ops:
  7.2 166.5 %all-gather.11.cloned.1.call-start = ((), (), s32[]{:S(2)}) async-start(), calls=%async_computation | async-start | bytes 5283840 | tf_op jit(solution)/shard_map/all_gather | solution.py:93
  30.5 14.6 %collective-permute-start.5 = (f32[16,4,1,128]{3,0,2,1:T(8,128)S(1)}, f32[16,4,1,128]{3,0,2,1:T(8,128)S(1)}, u32[]{:S(2)}, u32[]{:S(2)}) collective-permute-start(f32[16,4,1,128]{3,0,2,1:T(8,128)S(1)} %get-tuple-element.125), channel_id=1, source_target_pairs={{0,8},{8,16},{16,24},{24,32},{32,40},{40,48},{48,56},{56,64},{64,7... | collective-permute-start | bytes 98312 | tf_op jit(solution)/shard_map/ppermute | solution.py:33
  33.7 11.4 %collective-permute-start.6 = (f32[16,4,1,128]{3,0,2,1:T(8,128)S(1)}, f32[16,4,1,128]{3,0,2,1:T(8,128)S(1)}, u32[]{:S(2)}, u32[]{:S(2)}) collective-permute-start(f32[16,4,1,128]{3,0,2,1:T(8,128)S(1)} %get-tuple-element.126), channel_id=1, source_target_pairs={{8,0},{16,8},{24,16},{32,24},{40,32},{48,40},{56,48},{64,56},{72,6... | collective-permute-start | bytes 98312 | tf_op jit(solution)/shard_map/ppermute | solution.py:33
  37.3 7.7 collective-permute-start.7
  45.9 15.5 %collective-permute-start.9 = (f32[16,4,1,128]{3,0,2,1:T(8,128)S(1)}, f32[16,4,1,128]{3,0,2,1:T(8,128)S(1)}, u32[]{:S(2)}, u32[]{:S(2)}) collective-permute-start(f32[16,4,1,128]{3,0,2,1:T(8,128)S(1)} %get-tuple-element.121), channel_id=1, source_target_pairs={{0,8},{8,16},{16,24},{24,32},{32,40},{40,48},{48,56},{56,64},{64,7... | collective-permute-start | bytes 98312 | tf_op jit(solution)/shard_map/ppermute | solution.py:33
  50.2 11.2 %collective-permute-start.10 = (f32[16,4,1,128]{3,0,2,1:T(8,128)S(1)}, f32[16,4,1,128]{3,0,2,1:T(8,128)S(1)}, u32[]{:S(2)}, u32[]{:S(2)}) collective-permute-start(f32[16,4,1,128]{3,0,2,1:T(8,128)S(1)} %get-tuple-element.122), channel_id=1, source_target_pairs={{8,0},{16,8},{24,16},{32,24},{40,32},{48,40},{56,48},{64,56},{72,6... | collective-permute-start | bytes 98312 | tf_op jit(solution)/shard_map/ppermute | solution.py:33
  53.6 7.7 collective-permute-start.11
  62.2 16.4 %collective-permute-start.13 = (f32[16,4,1,128]{3,0,2,1:T(8,128)S(1)}, f32[16,4,1,128]{3,0,2,1:T(8,128)S(1)}, u32[]{:S(2)}, u32[]{:S(2)}) collective-permute-start(f32[16,4,1,128]{3,0,2,1:T(8,128)S(1)} %get-tuple-element.117), channel_id=1, source_target_pairs={{0,8},{8,16},{16,24},{24,32},{32,40},{40,48},{48,56},{56,64},{64,7... | collective-permute-start | bytes 98312 | tf_op jit(solution)/shard_map/ppermute | solution.py:33
  67.4 11.2 %collective-permute-start.14 = (f32[16,4,1,128]{3,0,2,1:T(8,128)S(1)}, f32[16,4,1,128]{3,0,2,1:T(8,128)S(1)}, u32[]{:S(2)}, u32[]{:S(2)}) collective-permute-start(f32[16,4,1,128]{3,0,2,1:T(8,128)S(1)} %get-tuple-element.118), channel_id=1, source_target_pairs={{8,0},{16,8},{24,16},{32,24},{40,32},{48,40},{56,48},{64,56},{72,6... | collective-permute-start | bytes 98312 | tf_op jit(solution)/shard_map/ppermute | solution.py:33
  70.9 7.7 collective-permute-start.15
  79.4 15.5 %collective-permute-start.17 = (f32[16,4,1,128]{3,0,2,1:T(8,128)S(1)}, f32[16,4,1,128]{3,0,2,1:T(8,128)S(1)}, u32[]{:S(2)}, u32[]{:S(2)}) collective-permute-start(f32[16,4,1,128]{3,0,2,1:T(8,128)S(1)} %get-tuple-element.113), channel_id=1, source_target_pairs={{0,8},{8,16},{16,24},{24,32},{32,40},{40,48},{48,56},{56,64},{64,7... | collective-permute-start | bytes 98312 | tf_op jit(solution)/shard_map/ppermute | solution.py:33
  83.7 11.2 %collective-permute-start.18 = (f32[16,4,1,128]{3,0,2,1:T(8,128)S(1)}, f32[16,4,1,128]{3,0,2,1:T(8,128)S(1)}, u32[]{:S(2)}, u32[]{:S(2)}) collective-permute-start(f32[16,4,1,128]{3,0,2,1:T(8,128)S(1)} %get-tuple-element.114), channel_id=1, source_target_pairs={{8,0},{16,8},{24,16},{32,24},{40,32},{48,40},{56,48},{64,56},{72,6... | collective-permute-start | bytes 98312 | tf_op jit(solution)/shard_map/ppermute | solution.py:33
  87.2 7.7 collective-permute-start.19
  97.5 235.9 %all-gather.13.cloned.1.call-start = ((), (), s32[]{:S(2)}) async-start(), calls=%async_computation.1 | async-start | bytes 5283840 | tf_op jit(solution)/shard_map/all_gather | solution.py:93
  192.9 13.7 %collective-permute-start.21 = (f32[16,4,1,128]{3,0,2,1:T(8,128)S(1)}, f32[16,4,1,128]{3,0,2,1:T(8,128)S(1)}, u32[]{:S(2)}, u32[]{:S(2)}) collective-permute-start(f32[16,4,1,128]{3,0,2,1:T(8,128)S(1)} %get-tuple-element.109), channel_id=1, source_target_pairs={{0,8},{8,16},{16,24},{24,32},{32,40},{40,48},{48,56},{56,64},{64,7... | collective-permute-start | bytes 98312 | tf_op jit(solution)/shard_map/ppermute | solution.py:33
  194.7 11.9 %collective-permute-start.22 = (f32[16,4,1,128]{3,0,2,1:T(8,128)S(1)}, f32[16,4,1,128]{3,0,2,1:T(8,128)S(1)}, u32[]{:S(2)}, u32[]{:S(2)}) collective-permute-start(f32[16,4,1,128]{3,0,2,1:T(8,128)S(1)} %get-tuple-element.110), channel_id=1, source_target_pairs={{8,0},{16,8},{24,16},{32,24},{40,32},{48,40},{56,48},{64,56},{72,6... | collective-permute-start | bytes 98312 | tf_op jit(solution)/shard_map/ppermute | solution.py:33
  198.9 7.7 collective-permute-start.23
  207.4 15.5 %collective-permute-start.25 = (f32[16,4,1,128]{3,0,2,1:T(8,128)S(1)}, f32[16,4,1,128]{3,0,2,1:T(8,128)S(1)}, u32[]{:S(2)}, u32[]{:S(2)}) collective-permute-start(f32[16,4,1,128]{3,0,2,1:T(8,128)S(1)} %get-tuple-element.105), channel_id=1, source_target_pairs={{0,8},{8,16},{16,24},{24,32},{32,40},{40,48},{48,56},{56,64},{64,7... | collective-permute-start | bytes 98312 | tf_op jit(solution)/shard_map/ppermute | solution.py:33
  211.7 11.2 %collective-permute-start.26 = (f32[16,4,1,128]{3,0,2,1:T(8,128)S(1)}, f32[16,4,1,128]{3,0,2,1:T(8,128)S(1)}, u32[]{:S(2)}, u32[]{:S(2)}) collective-permute-start(f32[16,4,1,128]{3,0,2,1:T(8,128)S(1)} %get-tuple-element.106), channel_id=1, source_target_pairs={{8,0},{16,8},{24,16},{32,24},{40,32},{48,40},{56,48},{64,56},{72,6... | collective-permute-start | bytes 98312 | tf_op jit(solution)/shard_map/ppermute | solution.py:33
  215.2 7.7 collective-permute-start.27
  223.7 15.5 %collective-permute-start.29 = (f32[16,4,1,128]{3,0,2,1:T(8,128)S(1)}, f32[16,4,1,128]{3,0,2,1:T(8,128)S(1)}, u32[]{:S(2)}, u32[]{:S(2)}) collective-permute-start(f32[16,4,1,128]{3,0,2,1:T(8,128)S(1)} %get-tuple-element.101), channel_id=1, source_target_pairs={{0,8},{8,16},{16,24},{24,32},{32,40},{40,48},{48,56},{56,64},{64,7... | collective-permute-start | bytes 98312 | tf_op jit(solution)/shard_map/ppermute | solution.py:33
  228.0 11.2 %collective-permute-start.30 = (f32[16,4,1,128]{3,0,2,1:T(8,128)S(1)}, f32[16,4,1,128]{3,0,2,1:T(8,128)S(1)}, u32[]{:S(2)}, u32[]{:S(2)}) collective-permute-start(f32[16,4,1,128]{3,0,2,1:T(8,128)S(1)} %get-tuple-element.102), channel_id=1, source_target_pairs={{8,0},{16,8},{24,16},{32,24},{40,32},{48,40},{56,48},{64,56},{72,6... | collective-permute-start | bytes 98312 | tf_op jit(solution)/shard_map/ppermute | solution.py:33
  231.5 7.7 collective-permute-start.31
  240.0 15.5 %collective-permute-start.33 = (f32[16,4,1,128]{3,0,2,1:T(8,128)S(1)}, f32[16,4,1,128]{3,0,2,1:T(8,128)S(1)}, u32[]{:S(2)}, u32[]{:S(2)}) collective-permute-start(f32[16,4,1,128]{3,0,2,1:T(8,128)S(1)} %get-tuple-element.97), channel_id=1, source_target_pairs={{0,8},{8,16},{16,24},{24,32},{32,40},{40,48},{48,56},{56,64},{64,7... | collective-permute-start | bytes 98312 | tf_op jit(solution)/shard_map/ppermute | solution.py:33
  244.3 11.2 %collective-permute-start.34 = (f32[16,4,1,128]{3,0,2,1:T(8,128)S(1)}, f32[16,4,1,128]{3,0,2,1:T(8,128)S(1)}, u32[]{:S(2)}, u32[]{:S(2)}) collective-permute-start(f32[16,4,1,128]{3,0,2,1:T(8,128)S(1)} %get-tuple-element.98), channel_id=1, source_target_pairs={{8,0},{16,8},{24,16},{32,24},{40,32},{48,40},{56,48},{64,56},{72,6... | collective-permute-start | bytes 98312 | tf_op jit(solution)/shard_map/ppermute | solution.py:33
  247.8 7.7 collective-permute-start.35
  258.1 235.1 %all-gather.15.cloned.1.call-start = ((), (), s32[]{:S(2)}) async-start(), calls=%async_computation.2 | async-start | bytes 5283840 | tf_op jit(solution)/shard_map/all_gather | solution.py:93
  352.7 13.7 %collective-permute-start.37 = (f32[16,4,1,128]{3,0,2,1:T(8,128)S(1)}, f32[16,4,1,128]{3,0,2,1:T(8,128)S(1)}, u32[]{:S(2)}, u32[]{:S(2)}) collective-permute-start(f32[16,4,1,128]{3,0,2,1:T(8,128)S(1)} %get-tuple-element.93), channel_id=1, source_target_pairs={{0,8},{8,16},{16,24},{24,32},{32,40},{40,48},{48,56},{56,64},{64,7... | collective-permute-start | bytes 98312 | tf_op jit(solution)/shard_map/ppermute | solution.py:33
  354.5 11.9 %collective-permute-start.38 = (f32[16,4,1,128]{3,0,2,1:T(8,128)S(1)}, f32[16,4,1,128]{3,0,2,1:T(8,128)S(1)}, u32[]{:S(2)}, u32[]{:S(2)}) collective-permute-start(f32[16,4,1,128]{3,0,2,1:T(8,128)S(1)} %get-tuple-element.94), channel_id=1, source_target_pairs={{8,0},{16,8},{24,16},{32,24},{40,32},{48,40},{56,48},{64,56},{72,6... | collective-permute-start | bytes 98312 | tf_op jit(solution)/shard_map/ppermute | solution.py:33
  358.7 7.7 collective-permute-start.39
  367.2 15.5 %collective-permute-start.41 = (f32[16,4,1,128]{3,0,2,1:T(8,128)S(1)}, f32[16,4,1,128]{3,0,2,1:T(8,128)S(1)}, u32[]{:S(2)}, u32[]{:S(2)}) collective-permute-start(f32[16,4,1,128]{3,0,2,1:T(8,128)S(1)} %get-tuple-element.89), channel_id=1, source_target_pairs={{0,8},{8,16},{16,24},{24,32},{32,40},{40,48},{48,56},{56,64},{64,7... | collective-permute-start | bytes 98312 | tf_op jit(solution)/shard_map/ppermute | solution.py:33
  371.5 11.2 %collective-permute-start.42 = (f32[16,4,1,128]{3,0,2,1:T(8,128)S(1)}, f32[16,4,1,128]{3,0,2,1:T(8,128)S(1)}, u32[]{:S(2)}, u32[]{:S(2)}) collective-permute-start(f32[16,4,1,128]{3,0,2,1:T(8,128)S(1)} %get-tuple-element.90), channel_id=1, source_target_pairs={{8,0},{16,8},{24,16},{32,24},{40,32},{48,40},{56,48},{64,56},{72,6... | collective-permute-start | bytes 98312 | tf_op jit(solution)/shard_map/ppermute | solution.py:33
  375.0 7.7 collective-permute-start.43
  383.5 15.5 %collective-permute-start.45 = (f32[16,4,1,128]{3,0,2,1:T(8,128)S(1)}, f32[16,4,1,128]{3,0,2,1:T(8,128)S(1)}, u32[]{:S(2)}, u32[]{:S(2)}) collective-permute-start(f32[16,4,1,128]{3,0,2,1:T(8,128)S(1)} %get-tuple-element.85), channel_id=1, source_target_pairs={{0,8},{8,16},{16,24},{24,32},{32,40},{40,48},{48,56},{56,64},{64,7... | collective-permute-start | bytes 98312 | tf_op jit(solution)/shard_map/ppermute | solution.py:33
  387.8 11.2 %collective-permute-start.46 = (f32[16,4,1,128]{3,0,2,1:T(8,128)S(1)}, f32[16,4,1,128]{3,0,2,1:T(8,128)S(1)}, u32[]{:S(2)}, u32[]{:S(2)}) collective-permute-start(f32[16,4,1,128]{3,0,2,1:T(8,128)S(1)} %get-tuple-element.86), channel_id=1, source_target_pairs={{8,0},{16,8},{24,16},{32,24},{40,32},{48,40},{56,48},{64,56},{72,6... | collective-permute-start | bytes 98312 | tf_op jit(solution)/shard_map/ppermute | solution.py:33
  391.3 7.7 collective-permute-start.47
  399.8 15.5 %collective-permute-start.49 = (f32[16,4,1,128]{3,0,2,1:T(8,128)S(1)}, f32[16,4,1,128]{3,0,2,1:T(8,128)S(1)}, u32[]{:S(2)}, u32[]{:S(2)}) collective-permute-start(f32[16,4,1,128]{3,0,2,1:T(8,128)S(1)} %get-tuple-element.81), channel_id=1, source_target_pairs={{0,8},{8,16},{16,24},{24,32},{32,40},{40,48},{48,56},{56,64},{64,7... | collective-permute-start | bytes 98312 | tf_op jit(solution)/shard_map/ppermute | solution.py:33
  404.1 11.2 %collective-permute-start.50 = (f32[16,4,1,128]{3,0,2,1:T(8,128)S(1)}, f32[16,4,1,128]{3,0,2,1:T(8,128)S(1)}, u32[]{:S(2)}, u32[]{:S(2)}) collective-permute-start(f32[16,4,1,128]{3,0,2,1:T(8,128)S(1)} %get-tuple-element.82), channel_id=1, source_target_pairs={{8,0},{16,8},{24,16},{32,24},{40,32},{48,40},{56,48},{64,56},{72,6... | collective-permute-start | bytes 98312 | tf_op jit(solution)/shard_map/ppermute | solution.py:33
  407.6 7.7 collective-permute-start.51
  417.9 235.1 %all-gather.17.cloned.1.call-start = ((), (), s32[]{:S(2)}) async-start(), calls=%async_computation.3 | async-start | bytes 5283840 | tf_op jit(solution)/shard_map/all_gather | solution.py:93
  512.5 13.7 %collective-permute-start.53 = (f32[16,4,1,128]{3,0,2,1:T(8,128)S(1)}, f32[16,4,1,128]{3,0,2,1:T(8,128)S(1)}, u32[]{:S(2)}, u32[]{:S(2)}) collective-permute-start(f32[16,4,1,128]{3,0,2,1:T(8,128)S(1)} %get-tuple-element.77), channel_id=1, source_target_pairs={{0,8},{8,16},{16,24},{24,32},{32,40},{40,48},{48,56},{56,64},{64,7... | collective-permute-start | bytes 98312 | tf_op jit(solution)/shard_map/ppermute | solution.py:33
  514.3 11.9 %collective-permute-start.54 = (f32[16,4,1,128]{3,0,2,1:T(8,128)S(1)}, f32[16,4,1,128]{3,0,2,1:T(8,128)S(1)}, u32[]{:S(2)}, u32[]{:S(2)}) collective-permute-start(f32[16,4,1,128]{3,0,2,1:T(8,128)S(1)} %get-tuple-element.78), channel_id=1, source_target_pairs={{8,0},{16,8},{24,16},{32,24},{40,32},{48,40},{56,48},{64,56},{72,6... | collective-permute-start | bytes 98312 | tf_op jit(solution)/shard_map/ppermute | solution.py:33
  518.5 7.7 collective-permute-start.55
  527.0 15.5 %collective-permute-start.57 = (f32[16,4,1,128]{3,0,2,1:T(8,128)S(1)}, f32[16,4,1,128]{3,0,2,1:T(8,128)S(1)}, u32[]{:S(2)}, u32[]{:S(2)}) collective-permute-start(f32[16,4,1,128]{3,0,2,1:T(8,128)S(1)} %get-tuple-element.73), channel_id=1, source_target_pairs={{0,8},{8,16},{16,24},{24,32},{32,40},{40,48},{48,56},{56,64},{64,7... | collective-permute-start | bytes 98312 | tf_op jit(solution)/shard_map/ppermute | solution.py:33
  531.3 11.2 %collective-permute-start.58 = (f32[16,4,1,128]{3,0,2,1:T(8,128)S(1)}, f32[16,4,1,128]{3,0,2,1:T(8,128)S(1)}, u32[]{:S(2)}, u32[]{:S(2)}) collective-permute-start(f32[16,4,1,128]{3,0,2,1:T(8,128)S(1)} %get-tuple-element.74), channel_id=1, source_target_pairs={{8,0},{16,8},{24,16},{32,24},{40,32},{48,40},{56,48},{64,56},{72,6... | collective-permute-start | bytes 98312 | tf_op jit(solution)/shard_map/ppermute | solution.py:33
  534.8 7.7 collective-permute-start.59
  543.3 15.5 %collective-permute-start.61 = (f32[16,4,1,128]{3,0,2,1:T(8,128)S(1)}, f32[16,4,1,128]{3,0,2,1:T(8,128)S(1)}, u32[]{:S(2)}, u32[]{:S(2)}) collective-permute-start(f32[16,4,1,128]{3,0,2,1:T(8,128)S(1)} %get-tuple-element.69), channel_id=1, source_target_pairs={{0,8},{8,16},{16,24},{24,32},{32,40},{40,48},{48,56},{56,64},{64,7... | collective-permute-start | bytes 98312 | tf_op jit(solution)/shard_map/ppermute | solution.py:33
  547.6 11.2 %collective-permute-start.62 = (f32[16,4,1,128]{3,0,2,1:T(8,128)S(1)}, f32[16,4,1,128]{3,0,2,1:T(8,128)S(1)}, u32[]{:S(2)}, u32[]{:S(2)}) collective-permute-start(f32[16,4,1,128]{3,0,2,1:T(8,128)S(1)} %get-tuple-element.70), channel_id=1, source_target_pairs={{8,0},{16,8},{24,16},{32,24},{40,32},{48,40},{56,48},{64,56},{72,6... | collective-permute-start | bytes 98312 | tf_op jit(solution)/shard_map/ppermute | solution.py:33
  551.1 7.7 collective-permute-start.63
  559.6 15.5 %collective-permute-start.65 = (f32[16,4,1,128]{3,0,2,1:T(8,128)S(1)}, f32[16,4,1,128]{3,0,2,1:T(8,128)S(1)}, u32[]{:S(2)}, u32[]{:S(2)}) collective-permute-start(f32[16,4,1,128]{3,0,2,1:T(8,128)S(1)} %get-tuple-element.65), channel_id=1, source_target_pairs={{0,8},{8,16},{16,24},{24,32},{32,40},{40,48},{48,56},{56,64},{64,7... | collective-permute-start | bytes 98312 | tf_op jit(solution)/shard_map/ppermute | solution.py:33
  563.9 11.2 %collective-permute-start.66 = (f32[16,4,1,128]{3,0,2,1:T(8,128)S(1)}, f32[16,4,1,128]{3,0,2,1:T(8,128)S(1)}, u32[]{:S(2)}, u32[]{:S(2)}) collective-permute-start(f32[16,4,1,128]{3,0,2,1:T(8,128)S(1)} %get-tuple-element.66), channel_id=1, source_target_pairs={{8,0},{16,8},{24,16},{32,24},{40,32},{48,40},{56,48},{64,56},{72,6... | collective-permute-start | bytes 98312 | tf_op jit(solution)/shard_map/ppermute | solution.py:33
  567.4 7.7 collective-permute-start.67
  577.7 235.5 %all-gather.19.cloned.1.call-start = ((), (), s32[]{:S(2)}) async-start(), calls=%async_computation.4 | async-start | bytes 5283840 | tf_op jit(solution)/shard_map/all_gather | solution.py:93
  672.6 13.7 %collective-permute-start.69 = (f32[16,4,1,128]{3,0,2,1:T(8,128)S(1)}, f32[16,4,1,128]{3,0,2,1:T(8,128)S(1)}, u32[]{:S(2)}, u32[]{:S(2)}) collective-permute-start(f32[16,4,1,128]{3,0,2,1:T(8,128)S(1)} %get-tuple-element.61), channel_id=1, source_target_pairs={{0,8},{8,16},{16,24},{24,32},{32,40},{40,48},{48,56},{56,64},{64,7... | collective-permute-start | bytes 98312 | tf_op jit(solution)/shard_map/ppermute | solution.py:33
  674.4 11.9 %collective-permute-start.70 = (f32[16,4,1,128]{3,0,2,1:T(8,128)S(1)}, f32[16,4,1,128]{3,0,2,1:T(8,128)S(1)}, u32[]{:S(2)}, u32[]{:S(2)}) collective-permute-start(f32[16,4,1,128]{3,0,2,1:T(8,128)S(1)} %get-tuple-element.62), channel_id=1, source_target_pairs={{8,0},{16,8},{24,16},{32,24},{40,32},{48,40},{56,48},{64,56},{72,6... | collective-permute-start | bytes 98312 | tf_op jit(solution)/shard_map/ppermute | solution.py:33
  678.6 7.7 collective-permute-start.71
  687.2 15.5 %collective-permute-start.73 = (f32[16,4,1,128]{3,0,2,1:T(8,128)S(1)}, f32[16,4,1,128]{3,0,2,1:T(8,128)S(1)}, u32[]{:S(2)}, u32[]{:S(2)}) collective-permute-start(f32[16,4,1,128]{3,0,2,1:T(8,128)S(1)} %get-tuple-element.57), channel_id=1, source_target_pairs={{0,8},{8,16},{16,24},{24,32},{32,40},{40,48},{48,56},{56,64},{64,7... | collective-permute-start | bytes 98312 | tf_op jit(solution)/shard_map/ppermute | solution.py:33
  691.5 11.2 %collective-permute-start.74 = (f32[16,4,1,128]{3,0,2,1:T(8,128)S(1)}, f32[16,4,1,128]{3,0,2,1:T(8,128)S(1)}, u32[]{:S(2)}, u32[]{:S(2)}) collective-permute-start(f32[16,4,1,128]{3,0,2,1:T(8,128)S(1)} %get-tuple-element.58), channel_id=1, source_target_pairs={{8,0},{16,8},{24,16},{32,24},{40,32},{48,40},{56,48},{64,56},{72,6... | collective-permute-start | bytes 98312 | tf_op jit(solution)/shard_map/ppermute | solution.py:33
  694.9 7.7 collective-permute-start.75
  703.5 15.5 %collective-permute-start.77 = (f32[16,4,1,128]{3,0,2,1:T(8,128)S(1)}, f32[16,4,1,128]{3,0,2,1:T(8,128)S(1)}, u32[]{:S(2)}, u32[]{:S(2)}) collective-permute-start(f32[16,4,1,128]{3,0,2,1:T(8,128)S(1)} %get-tuple-element.53), channel_id=1, source_target_pairs={{0,8},{8,16},{16,24},{24,32},{32,40},{40,48},{48,56},{56,64},{64,7... | collective-permute-start | bytes 98312 | tf_op jit(solution)/shard_map/ppermute | solution.py:33
  707.8 11.2 %collective-permute-start.78 = (f32[16,4,1,128]{3,0,2,1:T(8,128)S(1)}, f32[16,4,1,128]{3,0,2,1:T(8,128)S(1)}, u32[]{:S(2)}, u32[]{:S(2)}) collective-permute-start(f32[16,4,1,128]{3,0,2,1:T(8,128)S(1)} %get-tuple-element.54), channel_id=1, source_target_pairs={{8,0},{16,8},{24,16},{32,24},{40,32},{48,40},{56,48},{64,56},{72,6... | collective-permute-start | bytes 98312 | tf_op jit(solution)/shard_map/ppermute | solution.py:33
  719.8 15.5 %collective-permute-start.81 = (f32[16,4,1,128]{3,0,2,1:T(8,128)S(1)}, f32[16,4,1,128]{3,0,2,1:T(8,128)S(1)}, u32[]{:S(2)}, u32[]{:S(2)}) collective-permute-start(f32[16,4,1,128]{3,0,2,1:T(8,128)S(1)} %get-tuple-element.49), channel_id=1, source_target_pairs={{0,8},{8,16},{16,24},{24,32},{32,40},{40,48},{48,56},{56,64},{64,7... | collective-permute-start | bytes 98312 | tf_op jit(solution)/shard_map/ppermute | solution.py:33
  724.1 11.2 %collective-permute-start.82 = (f32[16,4,1,128]{3,0,2,1:T(8,128)S(1)}, f32[16,4,1,128]{3,0,2,1:T(8,128)S(1)}, u32[]{:S(2)}, u32[]{:S(2)}) collective-permute-start(f32[16,4,1,128]{3,0,2,1:T(8,128)S(1)} %get-tuple-element.50), channel_id=1, source_target_pairs={{8,0},{16,8},{24,16},{32,24},{40,32},{48,40},{56,48},{64,56},{72,6... | collective-permute-start | bytes 98312 | tf_op jit(solution)/shard_map/ppermute | solution.py:33
  727.5 7.7 collective-permute-start.83
  (51 other events, 378.3 us)
Sparse Core Ops, SparseCore 0:
  97.6 75.9 all-gather.10
  258.2 75.1 all-gather.12
  418.0 75.1 all-gather.14
  577.8 75.1 all-gather.16
  738.0 75.1 all-gather.18
